TPU v7x, 32 devices: a whole 2x2x4 slice. The times are simulated.
32 devices in a mesh: mem: 8 (over z, core), slab: 4 (over y, x).
Axes of the slice: x: 2, y: 2, z: 4, core: 2. Of those that a mesh axis runs over, the one named last changes fastest.
Arguments:
- thickness: float32 [64, 256, 384], P('mem', 'slab'), may hold values from 0.5 to 2.5
- face_u: float32 [256, 384], P('slab'), may hold values from -0.4 to 0.4
- face_v: float32 [256, 384], P('slab'), may hold values from -0.4 to 0.4
- obs_cells: int32 [512, 4], P('slab'), may hold values from 0 to 98303, as said below
- obs_weights: int32 [512, 4], P('slab'), may hold values from 1 to 4
- obs_values: float32 [512], P('slab'), may hold values from -6 to 6
- obs_noise: float32 [64, 512], P('mem', 'slab'), may hold values from -3 to 3
- cov_inverse: float32 [512, 512], P('slab'), may hold values from -0.375 to 0.375
- taper_mask: int32 [4, 4], replicated, may hold values from 0 to 1, as said below
Outputs:
- analysis: float32 [64, 256, 384], P('mem', 'slab')
Inputs may be any that keep to these rules, and one draw needn't show every extreme that they name: `obs_cells`: observation o covers a 2 x 2 square of cells, all within the rows of slab o // 128. `taper_mask`: entries are 0 or 1 and the diagonal is 1.
All inputs are finite; a program needn't handle non-finite values.
Results may differ from a plain program's by a relative error of at most 0.0003.
Values sent between devices are 32-bit elements; how exact they have to be, the bound alone decides.
A program may use at most 64 MiB of HBM per device.

v0:
```python
import jax
import jax.numpy as jnp
from jax import lax
from jax.sharding import PartitionSpec as P


def padded_2(block, sides, width):
    for axis, dim in sides:
        count = lax.axis_size(axis)
        forward = [(i, i + 1) for i in range(count - 1)]
        backward = [(target, source) for source, target in forward]
        low = lax.ppermute(
            lax.slice_in_dim(block, block.shape[dim] - width, None, axis=dim), axis, forward
        )
        high = lax.ppermute(lax.slice_in_dim(block, 0, width, axis=dim), axis, backward)
        block = jnp.concatenate([low, block, high], axis=dim)
    return block


def minmod(first_diff, second_diff):
    return (
        0.5
        * (jnp.sign(first_diff) + jnp.sign(second_diff))
        * jnp.minimum(jnp.abs(first_diff), jnp.abs(second_diff))
    )


def face_flux(padded, velocity, axis_dim):
    counted = padded.shape[axis_dim] - 3
    far_low = lax.slice_in_dim(padded, 0, counted, axis=axis_dim)
    near_low = lax.slice_in_dim(padded, 1, 1 + counted, axis=axis_dim)
    near_high = lax.slice_in_dim(padded, 2, 2 + counted, axis=axis_dim)
    far_high = lax.slice_in_dim(padded, 3, 3 + counted, axis=axis_dim)
    left_state = near_low + 0.5 * minmod(near_low - far_low, near_high - near_low)
    right_state = near_high - 0.5 * minmod(near_high - near_low, far_high - near_high)
    return jnp.maximum(velocity, 0.0) * left_state + jnp.minimum(velocity, 0.0) * right_state


def local(
    thickness,
    face_u,
    face_v,
    obs_cells,
    obs_weights,
    obs_values,
    obs_noise,
    cov_inverse,
    taper_mask,
):
    member_subset = thickness.shape[0]
    band_rows = thickness.shape[1]
    column_list = thickness.shape[2]
    slab_index = lax.axis_index("slab")
    stacked = jnp.concatenate([thickness, face_v[None]], 0)
    padded = padded_2(stacked, (("slab", 1),), 2)
    row_pad = padded[:member_subset]
    row_speed = padded[member_subset, 2 : band_rows + 3]
    row_fluxes = face_flux(row_pad, row_speed, 1)
    col_pad = jnp.pad(thickness, ((0, 0), (0, 0), (2, 2)))
    col_speed = jnp.pad(face_u, ((0, 0), (0, 1)))
    column_fluxes = face_flux(col_pad, col_speed, 2)
    prior_state = (
        thickness
        - (column_fluxes[:, :, 1:] - column_fluxes[:, :, :-1])
        - (row_fluxes[:, 1:, :] - row_fluxes[:, :-1, :])
    )
    state_vector = prior_state.reshape(member_subset, band_rows * column_list)
    local_cells = obs_cells - slab_index * (band_rows * column_list)
    weights = obs_weights.astype(jnp.float32)
    picked = state_vector[:, local_cells]
    obs_model = jnp.sum(picked * weights[None], -1) / jnp.sum(weights, -1)[None]
    innovation = obs_values[None, :] + obs_noise - obs_model
    white_terms = jnp.dot(innovation, cov_inverse, precision=lax.Precision.HIGHEST)
    whitened = lax.psum_scatter(white_terms, "slab", scatter_dimension=1, tiled=True)
    model_all, white_all = (
        lax.all_gather(obs_model, "mem", axis=0, tiled=True),
        lax.all_gather(whitened, "mem", axis=0, tiled=True),
    )
    obs_mean = jnp.mean(model_all, 0, keepdims=True)
    cell_state = lax.all_to_all(state_vector, "mem", split_axis=1, concat_axis=0, tiled=True)
    members = cell_state.shape[0]
    anomaly = cell_state - jnp.mean(cell_state, 0, keepdims=True)
    obs_anomaly = model_all - obs_mean
    anom_full, white_full = (
        lax.all_gather(obs_anomaly, "slab", axis=1, tiled=True),
        lax.all_gather(white_all, "slab", axis=1, tiled=True),
    )
    block_size = obs_anomaly.shape[1]
    mask_row = lax.dynamic_slice_in_dim(taper_mask, slab_index, 1, 0)[0].astype(jnp.float32)
    taper_row = jnp.repeat(mask_row, block_size)
    cross = lax.dot_general(
        anomaly, anom_full, (((0,), (0,)), ((), ())), precision=lax.Precision.HIGHEST
    ) / (members - 1)
    tapered = cross * taper_row[None, :]
    update = lax.dot_general(
        white_full, tapered, (((1,), (1,)), ((), ())), precision=lax.Precision.HIGHEST
    )
    analysis_cells = cell_state + update
    returned = lax.all_to_all(analysis_cells, "mem", split_axis=0, concat_axis=1, tiled=True)
    return returned.reshape(member_subset, band_rows, column_list)


def solution(mesh):
    return jax.shard_map(
        local,
        mesh=mesh,
        in_specs=(
            P("mem", "slab", None),
            P("slab", None),
            P("slab", None),
            P("slab", None),
            P("slab", None),
            P("slab"),
            P("mem", "slab"),
            P("slab", None),
            P(),
        ),
        out_specs=P("mem", "slab", None),
        check_vma=False,
    )
```

profile of v0, /device:TPU:0, one launch (start us, length us, event | category | flops | bytes accessed | tf_op | source)
XLA Modules:
  0.0 138.8 jit_solution(13175700690734752969)
XLA Ops:
  6.5 0.0 copy-start
  6.5 0.0 copy-start.1
  6.5 1.1 pad_maximum_fusion.3
  7.6 1.3 collective-permute-start
  8.9 5.5 %collective-permute-start.1 = (f32[9,2,384]{2,1,0:T(2,128)S(1)}, f32[9,2,384]{2,1,0:T(2,128)S(1)}, u32[]{:S(2)}, u32[]{:S(2)}) collective-permute-start(f32[9,2,384]{2,1,0:T(2,128)S(1)} %get-tuple-element.9), channel_id=1, source_target_pairs={{0,1},{1,2},{2,3},{4,5},{5,6},{6,7},{8,9},{9,10},{10,11},{12,13},{... | collective-permute-start | bytes 82952 | tf_op jit(solution)/shard_map/ppermute | solution.py:12
  14.4 0.9 pad_maximum_fusion.1
  15.4 0.7 compare_select_fusion
  16.1 0.1 copy.36
  16.2 0.1 reshape.37
  16.3 3.6 %multiply_add_fusion = f32[8,64,385]{2,1,0:T(8,128)S(1)} fusion(f32[8,64,384]{2,1,0:T(8,128)} %param.9, f32[64,385]{1,0:T(8,128)S(1)} %get-tuple-element.12, f32[64,385]{1,0:T(8,128)S(1)} %get-tuple-element.11), kind=kLoop, calls=%fused_computation.12 | loop fusion | flops 4730880 | bytes 1772032 | tf_op jit(solution)/shard_map/add | solution.py:36
  19.9 0.7 convert_reduce_fusion
  20.6 0.0 collective-permute-done
  20.6 0.9 maximum_bitcast_fusion
  21.6 0.0 collective-permute-done.1
  21.6 1.6 %maximum_maximum_fusion = (f32[9,66,384]{2,1,0:T(8,128)S(1)}, f32[9,66,384]{2,1,0:T(8,128)S(1)}) fusion(f32[1,64,384]{2,1,0:T(8,128)} %bitcast.30, f32[8,64,384]{2,1,0:T(8,128)} %param.9, f32[9,2,384]{2,1,0:T(2,128)S(1)} %collective-permute-done.1, f32[9,2,384]{2,1,0:T(2,128)S(1)} %collective-permute-done), kind=kLoop, calls=%fused_computation.14 | loop fusion | flops 912384 | bytes 2764800 | tf_op jit(solution)/shard_map/concatenate | solution.py:16
  23.2 0.0 copy-start.2
  23.2 1.3 multiply_add_fusion.1
  24.5 0.0 copy-done.1
  24.5 0.3 fusion.11
  24.9 0.1 all_to_all.26
  25.0 1.3 copy.34
  26.4 5.4 %all-to-all-start = ((f32[8,8,3072]{2,0,1:T(8,128)}), f32[8,8,3072]{2,0,1:T(8,128)S(1)}, u32[]{:S(2)}, u32[]{:S(2)}) async-start(f32[8,8,3072]{2,0,1:T(8,128)} %copy.34), calls=%async_computation | async-start | bytes 1572864 | tf_op jit(solution)/shard_map/all_to_all | solution.py:80
  31.8 0.0 reduce-scatter.2.cloned.1.call-start
  31.8 0.7 multiply_bitcast_fusion
  32.5 0.0 copy-done.2
  32.5 0.1 copy.37
  32.6 0.1 broadcast_bitcast_fusion
  32.7 0.0 copy-start.3
  32.7 0.0 copy-start.4
  32.7 6.6 %copy.35 = f32[8,64,384]{0,2,1:T(8,128)} copy(f32[8,64,384]{2,1,0:T(8,128)S(1)} %fusion.11) | data formatting | bytes 1572864 | tf_op jit(solution)/shard_map/sub | solution.py:63
  39.2 5.6 %gather_fusion = f32[512,8]{1,0:T(8,128)S(1)} fusion(f32[8,24576]{0,1:T(8,128)} %bitcast.25, s32[1024]{0:T(1024)S(1)} %pad_clamp_fusion), kind=kCustom, calls=%fused_computation | custom fusion | bytes 34816 | tf_op jit(solution)/shard_map/gather | solution.py:70
  44.9 0.2 multiply_reduce_fusion
  45.2 0.0 copy-done
  45.2 0.0 copy-done.3
  45.2 0.0 copy-done.4
  45.2 0.8 fusion.15
  46.0 0.0 reduce-scatter.2.cloned.1.call-update
  46.1 14.6 %all_gather.14 = f32[64,128]{1,0:T(8,128)S(1)} all-gather(f32[8,128]{1,0:T(8,128)S(1)} %divide_bitcast_fusion), channel_id=1, replica_groups=mesh['mem'=8,'slab'=4] {'mem'}, dimensions={0}, use_global_device_ids=true | all-gather | bytes 36864 | tf_op jit(solution)/shard_map/all_gather | solution.py:76
  60.7 9.9 %all_gather.15 = f32[64,512]{1,0:T(8,128)S(1)} all-gather(f32[64,128]{1,0:T(8,128)S(1)} %broadcast_subtract_fusion), channel_id=1, replica_groups=mesh['mem'=8,'slab'=4] {'slab'}, dimensions={1}, use_global_device_ids=true | all-gather | bytes 163840 | tf_op jit(solution)/shard_map/all_gather | solution.py:85
  70.6 0.0 reduce-scatter.2.cloned.1.call-done
  70.6 14.2 %all_gather.12 = f32[64,128]{1,0:T(8,128)S(1)} all-gather(f32[8,128]{1,0:T(8,128)} %reduce-scatter.2.cloned.1.call-done), channel_id=1, replica_groups=mesh['mem'=8,'slab'=4] {'mem'}, dimensions={0}, use_global_device_ids=true | all-gather | bytes 36864 | tf_op jit(solution)/shard_map/all_gather | solution.py:77
  84.7 9.0 %all_gather.13 = f32[64,512]{1,0:T(8,128)S(1)} all-gather(f32[64,128]{1,0:T(8,128)S(1)} %all_gather.12), channel_id=1, replica_groups=mesh['mem'=8,'slab'=4] {'slab'}, dimensions={1}, use_global_device_ids=true | all-gather | bytes 163840 | tf_op jit(solution)/shard_map/all_gather | solution.py:86
  93.8 0.0 all-to-all-done
  93.8 0.1 reduce_sum.38
  93.8 5.2 %fusion.13 = f32[3072,512]{1,0:T(8,128)S(1)} fusion(f32[64,512]{1,0:T(8,128)S(1)} %all_gather.15, f32[8,8,3072]{2,0,1:T(8,128)S(1)} %all-to-all-done, f32[3072]{0:T(1024)S(1)} %broadcast_multiply_fusion), kind=kOutput, calls=%fused_computation.23 | convolution fusion | flops 1208156160 | bytes 7221248 | tf_op jit(solution)/shard_map/dot_general | solution.py:91
  99.0 6.0 %fusion.5 = f32[8,8,3072]{2,1,0:T(8,128)S(1)} fusion(f32[64,512]{1,0:T(8,128)S(1)} %all_gather.13, f32[3072,512]{1,0:T(8,128)S(1)} %fusion.13, f32[512]{0:T(512)S(1)} %broadcast_bitcast_fusion, f32[8,8,3072]{2,0,1:T(8,128)S(1)} %all-to-all-done), kind=kOutput, calls=%fused_computation.4 | convolution fusion | flops 1209729024 | bytes 7997440 | tf_op jit(solution)/shard_map/dot_general | solution.py:95
  105.1 25.4 %all_to_all.35 = f32[8,8,3072]{2,1,0:T(8,128)S(1)} all-to-all(f32[8,8,3072]{2,1,0:T(8,128)S(1)} %fusion.5), channel_id=1, replica_groups=mesh['mem'=8,'slab'=4] {'mem'}, dimensions={0} | all-to-all | bytes 1572864 | tf_op jit(solution)/shard_map/all_to_all | solution.py:99
  130.5 0.5 copy.39
  130.9 1.0 reshape.34
  (9 shorter events, 0.1 us)
Async XLA Ops:
  6.5 38.6 %copy-start = (f32[128,512]{1,0:T(8,128)S(1)}, f32[128,512]{1,0:T(8,128)}, u32[]{:S(2)}) copy-start(f32[128,512]{1,0:T(8,128)} %param.16) | copy-start | bytes 786436
  6.5 18.0 %copy-start.1 = (f32[8,64,384]{2,1,0:T(8,128)S(1)}, f32[8,64,384]{2,1,0:T(8,128)}, u32[]{:S(2)}) copy-start(f32[8,64,384]{2,1,0:T(8,128)} %param.9) | copy-start | bytes 2359300
  7.6 13.0 %collective-permute-start = (f32[9,2,384]{2,1,0:T(2,128)S(1)}, f32[9,2,384]{2,1,0:T(2,128)S(1)}, u32[]{:S(2)}, u32[]{:S(2)}) collective-permute-start(f32[9,2,384]{2,1,0:T(2,128)S(1)} %get-tuple-element.10), channel_id=1, source_target_pairs={{1,0},{2,1},{3,2},{5,4},{6,5},{7,6},{9,8},{10,9},{11,10},{13,12},{... | collective-permute-start | bytes 82952 | tf_op jit(solution)/shard_map/ppermute | solution.py:15
  8.9 12.6 %collective-permute-start.1 = (f32[9,2,384]{2,1,0:T(2,128)S(1)}, f32[9,2,384]{2,1,0:T(2,128)S(1)}, u32[]{:S(2)}, u32[]{:S(2)}) collective-permute-start(f32[9,2,384]{2,1,0:T(2,128)S(1)} %get-tuple-element.9), channel_id=1, source_target_pairs={{0,1},{1,2},{2,3},{4,5},{5,6},{6,7},{8,9},{9,10},{10,11},{12,13},{... | collective-permute-start | bytes 82952 | tf_op jit(solution)/shard_map/ppermute | solution.py:12
  23.2 9.3 %copy-start.2 = (s32[128,4]{0,1:T(4,128)S(1)}, s32[128,4]{0,1:T(4,128)}, u32[]{:S(2)}) copy-start(s32[128,4]{0,1:T(4,128)} %param.13) | copy-start | bytes 6148
  26.4 67.4 %all-to-all-start = ((f32[8,8,3072]{2,0,1:T(8,128)}), f32[8,8,3072]{2,0,1:T(8,128)S(1)}, u32[]{:S(2)}, u32[]{:S(2)}) async-start(f32[8,8,3072]{2,0,1:T(8,128)} %copy.34), calls=%async_computation | async-start | bytes 1572864 | tf_op jit(solution)/shard_map/all_to_all | solution.py:80
  31.8 38.8 %reduce-scatter.2.cloned.1.call-start = ((), (), s32[]{:S(2)}) async-start(), calls=%async_computation.3 | async-start | bytes 20480 | tf_op jit(solution)/shard_map/reduce_scatter | solution.py:74
  32.7 12.5 %copy-start.3 = (f32[8,128]{1,0:T(8,128)S(1)}, f32[8,128]{1,0:T(8,128)}, u32[]{:S(2)}) copy-start(f32[8,128]{1,0:T(8,128)} %param.15) | copy-start | bytes 12292
  32.7 12.5 %copy-start.4 = (f32[128]{0:T(128)S(1)}, f32[128]{0:T(128)}, u32[]{:S(2)}) copy-start(f32[128]{0:T(128)} %param.14) | copy-start | bytes 1540
Sparse Core Ops, SparseCore 0:
  46.2 24.1 reduce-scatter.1
where the time goes:
time: 139 us
  blocking collectives  73 us (53%)
  local copies, waits for them, and re-layouts  15.6 us (11%)
  between operations  13.6 us (10%)
  other arithmetic  12.3 us (9%)
  starting transfers between devices  12.2 us (9%)
  matrix products  12.1 us (9%)
    all_to_all x1, blocking collectives, local(): lax.all_to_all(analysis_cells, 'mem', split_axis=0, concat_axis=1, tiled=...  25.4 us
    all_gather x1, blocking collectives, local(): lax.all_gather(obs_model, 'mem', axis=0, tiled=True)  14.6 us
    all_gather x1, blocking collectives, local(): lax.all_gather(whitened, 'mem', axis=0, tiled=True)  14.2 us
    all_gather x1, blocking collectives, local(): lax.all_gather(obs_anomaly, 'slab', axis=1, tiled=True)  9.86 us
    all_gather x1, blocking collectives, local(): lax.all_gather(white_all, 'slab', axis=1, tiled=True)  9 us
    sub x1, local copies, waits for them, and re-layouts, local(): thickness - (column_fluxes[:, :, 1:] - column_fluxes[:, :, :-1])  6.56 us
    dot_general x1, matrix products, local(): lax.dot_general(white_full, tapered, (((1,), (1,)), ((), ())), precision=...  6.04 us
    gather x1, local copies, waits for them, and re-layouts, local(): picked = state_vector[:, local_cells]  5.6 us
  transfers between devices with their start and end apart: 4, of which 0 were waited for; matrix products, arithmetic and copies ran while one was open for 15% of the time, Pallas kernels for 0%

commit v1 on v0

--- a/solution.py
+++ b/solution.py
@@ -96,7 +96,29 @@
         white_full, tapered, (((1,), (1,)), ((), ())), precision=lax.Precision.HIGHEST
     )
     analysis_cells = cell_state + update
-    returned = lax.all_to_all(analysis_cells, "mem", split_axis=0, concat_axis=1, tiled=True)
+
+    def switch_works(x_in, mesh_ax, d_out, dim_at):
+        big = lax.psum(1, mesh_ax)
+        local_out = lax.axis_index(mesh_ax)
+        piece_now, aux = (big, local_out)
+        far_arr = list(x_in.shape)
+        x_now = x_in.shape[d_out] // piece_now
+        far_arr[d_out] = x_now
+        y2 = far_arr[dim_at]
+        far_arr[dim_at] = y2 * piece_now
+        passed = jnp.zeros(far_arr, x_in.dtype)
+        for hop_no in [*range(piece_now)]:
+            state_next = lax.dynamic_slice_in_dim(x_in, (aux ^ hop_no) * x_now, x_now, axis=d_out)
+            if hop_no:
+                state_next = lax.ppermute(
+                    state_next, mesh_ax, [(num, num ^ hop_no) for num in range(piece_now)]
+                )
+            passed = lax.dynamic_update_slice_in_dim(
+                passed, state_next, (aux ^ hop_no) * y2, axis=dim_at
+            )
+        return passed
+
+    returned = switch_works(analysis_cells, "mem", 0, 1)
     return returned.reshape(member_subset, band_rows, column_list)
 
 

time: 139 us -> 135 us (0.971)
  the two profiles are of different devices: /device:TPU:0 before, /device:TPU:17 now
where the time goes in v1:
time: 135 us; the launch traced here: 134 us
  blocking collectives  40.8 us (30%)
  starting transfers between devices  21.3 us (16%)
  waiting for transfers between devices  18.8 us (14%)
  local copies, waits for them, and re-layouts  15.4 us (11%)
  between operations  13.7 us (10%)
  other arithmetic  12.2 us (9%)
  matrix products  12.1 us (9%)
    ppermute x7, waiting for transfers between devices, switch_works(): lax.ppermute(state_next, mesh_ax, [(num, num ^ hop_no) for num in range(p...  15.9 us
    all_gather x1, blocking collectives, local(): lax.all_gather(whitened, 'mem', axis=0, tiled=True)  13.5 us
    all_gather x1, blocking collectives, local(): lax.all_gather(obs_model, 'mem', axis=0, tiled=True)  12.5 us
    ppermute x7, starting transfers between devices, switch_works(): lax.ppermute(state_next, mesh_ax, [(num, num ^ hop_no) for num in range(p...  9.99 us
    all_gather x1, blocking collectives, local(): lax.all_gather(obs_anomaly, 'slab', axis=1, tiled=True)  7.83 us
    all_gather x1, blocking collectives, local(): lax.all_gather(white_all, 'slab', axis=1, tiled=True)  6.98 us
    sub x1, local copies, waits for them, and re-layouts, local(): thickness - (column_fluxes[:, :, 1:] - column_fluxes[:, :, :-1])  6.59 us
    all_to_all x1, starting transfers between devices, local(): lax.all_to_all(state_vector, 'mem', split_axis=1, concat_axis=0, tiled=True)  6.05 us
  transfers between devices with their start and end apart: 11, of which 6 were waited for; matrix products, arithmetic and copies ran while one was open for 16% of the time, Pallas kernels for 0%

profile of v1, /device:TPU:17, one launch (start us, length us, event | category | flops | bytes accessed | tf_op | source)
XLA Modules:
  0.0 134.3 jit_solution(2671326513478042009)
XLA Ops:
  6.5 0.0 copy-start
  6.5 0.0 copy-start.1
  6.5 1.1 pad_maximum_fusion.3
  7.6 1.3 collective-permute-start
  8.9 4.0 %collective-permute-start.1 = (f32[9,2,384]{2,1,0:T(2,128)S(1)}, f32[9,2,384]{2,1,0:T(2,128)S(1)}, u32[]{:S(2)}, u32[]{:S(2)}) collective-permute-start(f32[9,2,384]{2,1,0:T(2,128)S(1)} %get-tuple-element.9), channel_id=1, source_target_pairs={{0,1},{1,2},{2,3},{4,5},{5,6},{6,7},{8,9},{9,10},{10,11},{12,13},{... | collective-permute-start | bytes 82952 | tf_op jit(solution)/shard_map/ppermute | solution.py:12
  12.9 0.9 pad_maximum_fusion.1
  13.9 0.7 compare_select_fusion
  14.5 0.1 copy.32
  14.7 0.1 reshape.33
  14.8 3.6 %multiply_add_fusion = f32[8,64,385]{2,1,0:T(8,128)S(1)} fusion(f32[8,64,384]{2,1,0:T(8,128)} %param.9, f32[64,385]{1,0:T(8,128)S(1)} %get-tuple-element.20, f32[64,385]{1,0:T(8,128)S(1)} %get-tuple-element.19), kind=kLoop, calls=%fused_computation.11 | loop fusion | flops 4730880 | bytes 1772032 | tf_op jit(solution)/shard_map/add | solution.py:36
  18.4 0.7 convert_reduce_fusion
  19.1 0.0 collective-permute-done
  19.1 0.9 maximum_bitcast_fusion
  20.1 0.0 collective-permute-done.1
  20.1 1.6 %maximum_maximum_fusion = (f32[9,66,384]{2,1,0:T(8,128)S(1)}, f32[9,66,384]{2,1,0:T(8,128)S(1)}) fusion(f32[1,64,384]{2,1,0:T(8,128)} %bitcast.31, f32[8,64,384]{2,1,0:T(8,128)} %param.9, f32[9,2,384]{2,1,0:T(2,128)S(1)} %collective-permute-done.1, f32[9,2,384]{2,1,0:T(2,128)S(1)} %collective-permute-done), kind=kLoop, calls=%fused_computation.13 | loop fusion | flops 912384 | bytes 2764800 | tf_op jit(solution)/shard_map/concatenate | solution.py:16
  21.7 0.0 copy-start.2
  21.7 1.3 multiply_add_fusion.1
  23.0 0.0 copy-done.1
  23.0 0.3 fusion.8
  23.3 0.1 all_to_all.14
  23.5 1.3 copy.30
  24.8 6.1 %all-to-all-start = ((f32[8,8,3072]{2,0,1:T(8,128)}), f32[8,8,3072]{2,0,1:T(8,128)S(1)}, u32[]{:S(2)}, u32[]{:S(2)}) async-start(f32[8,8,3072]{2,0,1:T(8,128)} %copy.30), calls=%async_computation | async-start | bytes 1572864 | tf_op jit(solution)/shard_map/all_to_all | solution.py:80
  30.9 0.0 reduce-scatter.2.cloned.1.call-start
  30.9 0.7 fusion.18
  31.6 0.0 copy-done.2
  31.6 0.1 copy.33
  31.7 0.1 broadcast_bitcast_fusion
  31.8 0.0 copy-start.3
  31.8 0.0 copy-start.4
  31.8 6.6 %copy.31 = f32[8,64,384]{0,2,1:T(8,128)} copy(f32[8,64,384]{2,1,0:T(8,128)S(1)} %fusion.8) | data formatting | bytes 1572864 | tf_op jit(solution)/shard_map/sub | solution.py:63
  38.4 5.6 %gather_fusion = f32[512,8]{1,0:T(8,128)S(1)} fusion(f32[8,24576]{0,1:T(8,128)} %bitcast.26, s32[1024]{0:T(1024)S(1)} %pad_clamp_fusion), kind=kCustom, calls=%fused_computation | custom fusion | bytes 34816 | tf_op jit(solution)/shard_map/gather | solution.py:70
  44.0 0.2 multiply_reduce_fusion
  44.3 0.0 copy-done
  44.3 0.0 copy-done.3
  44.4 0.0 copy-done.4
  44.4 0.8 fusion.12
  45.2 0.0 reduce-scatter.2.cloned.1.call-update
  45.2 12.5 %all_gather.14 = f32[64,128]{1,0:T(8,128)S(1)} all-gather(f32[8,128]{1,0:T(8,128)S(1)} %divide_bitcast_fusion), channel_id=1, replica_groups=mesh['mem'=8,'slab'=4] {'mem'}, dimensions={0}, use_global_device_ids=true | all-gather | bytes 36864 | tf_op jit(solution)/shard_map/all_gather | solution.py:76
  57.8 7.8 %all_gather.15 = f32[64,512]{1,0:T(8,128)S(1)} all-gather(f32[64,128]{1,0:T(8,128)S(1)} %broadcast_subtract_fusion), channel_id=1, replica_groups=mesh['mem'=8,'slab'=4] {'slab'}, dimensions={1}, use_global_device_ids=true | all-gather | bytes 163840 | tf_op jit(solution)/shard_map/all_gather | solution.py:85
  65.6 2.9 %reduce-scatter.2.cloned.1.call-done = f32[8,128]{1,0:T(8,128)} async-done(((f32[8,512]{1,0:T(8,128)}), f32[8,128]{1,0:T(8,128)}) %reduce-scatter.2.cloned.1.call-update) | async-done | bytes 4112 | tf_op jit(solution)/shard_map/reduce_scatter | solution.py:74
  68.5 13.5 %all_gather.12 = f32[64,128]{1,0:T(8,128)S(1)} all-gather(f32[8,128]{1,0:T(8,128)} %reduce-scatter.2.cloned.1.call-done), channel_id=1, replica_groups=mesh['mem'=8,'slab'=4] {'mem'}, dimensions={0}, use_global_device_ids=true | all-gather | bytes 36864 | tf_op jit(solution)/shard_map/all_gather | solution.py:77
  82.0 7.0 %all_gather.13 = f32[64,512]{1,0:T(8,128)S(1)} all-gather(f32[64,128]{1,0:T(8,128)S(1)} %all_gather.12), channel_id=1, replica_groups=mesh['mem'=8,'slab'=4] {'slab'}, dimensions={1}, use_global_device_ids=true | all-gather | bytes 163840 | tf_op jit(solution)/shard_map/all_gather | solution.py:86
  88.9 0.0 all-to-all-done
  88.9 0.1 reduce_sum.38
  89.0 5.2 %fusion.10 = f32[3072,512]{1,0:T(8,128)S(1)} fusion(f32[64,512]{1,0:T(8,128)S(1)} %all_gather.15, f32[8,8,3072]{2,0,1:T(8,128)S(1)} %all-to-all-done, f32[3072]{0:T(1024)S(1)} %broadcast_multiply_fusion), kind=kOutput, calls=%fused_computation.23 | convolution fusion | flops 1208156160 | bytes 7221248 | tf_op jit(solution)/shard_map/dot_general | solution.py:91
  94.2 6.0 %fusion.2 = f32[64,3072]{1,0:T(8,128)S(1)} fusion(f32[64,512]{1,0:T(8,128)S(1)} %all_gather.13, f32[3072,512]{1,0:T(8,128)S(1)} %fusion.10, f32[512]{0:T(512)S(1)} %broadcast_bitcast_fusion, f32[8,8,3072]{2,0,1:T(8,128)S(1)} %all-to-all-done), kind=kOutput, calls=%fused_computation.3 | convolution fusion | flops 1209729024 | bytes 7997440 | tf_op jit(solution)/shard_map/dot_general | solution.py:95
  100.3 0.1 broadcast_in_dim.8
  100.3 0.1 constant_dynamic-slice_fusion
  100.4 2.3 %collective-permute-start.2 = (f32[8,3072]{1,0:T(8,128)S(1)}, f32[8,3072]{1,0:T(8,128)S(1)}, u32[]{:S(2)}, u32[]{:S(2)}) collective-permute-start(f32[8,3072]{1,0:T(8,128)S(1)} %get-tuple-element.17), channel_id=1, source_target_pairs={{0,4},{4,0},{8,12},{12,8},{16,20},{20,16},{24,28},{28,24},{1,5},{5... | collective-permute-start | bytes 294920 | tf_op jit(solution)/shard_map/ppermute | solution.py:113
  102.7 3.0 %collective-permute-start.3 = (f32[8,3072]{1,0:T(8,128)S(1)}, f32[8,3072]{1,0:T(8,128)S(1)}, u32[]{:S(2)}, u32[]{:S(2)}) collective-permute-start(f32[8,3072]{1,0:T(8,128)S(1)} %get-tuple-element.16), channel_id=1, source_target_pairs={{0,8},{4,12},{8,0},{12,4},{16,24},{20,28},{24,16},{28,20},{1,9},{5... | collective-permute-start | bytes 294920 | tf_op jit(solution)/shard_map/ppermute | solution.py:113
  105.6 0.1 collective-permute-start.4
  105.7 0.8 collective-permute-start.5
  106.5 2.1 %collective-permute-start.6 = (f32[8,3072]{1,0:T(8,128)S(1)}, f32[8,3072]{1,0:T(8,128)S(1)}, u32[]{:S(2)}, u32[]{:S(2)}) collective-permute-start(f32[8,3072]{1,0:T(8,128)S(1)} %get-tuple-element.13), channel_id=1, source_target_pairs={{0,20},{4,16},{8,28},{12,24},{16,4},{20,0},{24,12},{28,8},{1,21},{... | collective-permute-start | bytes 294920 | tf_op jit(solution)/shard_map/ppermute | solution.py:113
  108.6 0.0 collective-permute-done.2
  108.6 0.6 collective-permute-start.7
  109.2 0.0 collective-permute-done.3
  109.2 1.3 collective-permute-start.8
  110.4 0.7 collective-permute-done.4
  111.2 1.7 %collective-permute-done.5 = f32[8,3072]{1,0:T(8,128)S(1)} collective-permute-done((f32[8,3072]{1,0:T(8,128)S(1)}, f32[8,3072]{1,0:T(8,128)S(1)}, u32[]{:S(2)}, u32[]{:S(2)}) %collective-permute-start.5) | collective-permute-done | bytes 98336 | tf_op jit(solution)/shard_map/ppermute | solution.py:113
  112.9 6.7 %collective-permute-done.6 = f32[8,3072]{1,0:T(8,128)S(1)} collective-permute-done((f32[8,3072]{1,0:T(8,128)S(1)}, f32[8,3072]{1,0:T(8,128)S(1)}, u32[]{:S(2)}, u32[]{:S(2)}) %collective-permute-start.6) | collective-permute-done | bytes 98336 | tf_op jit(solution)/shard_map/ppermute | solution.py:113
  119.6 4.4 %collective-permute-done.7 = f32[8,3072]{1,0:T(8,128)S(1)} collective-permute-done((f32[8,3072]{1,0:T(8,128)S(1)}, f32[8,3072]{1,0:T(8,128)S(1)}, u32[]{:S(2)}, u32[]{:S(2)}) %collective-permute-start.7) | collective-permute-done | bytes 98336 | tf_op jit(solution)/shard_map/ppermute | solution.py:113
  124.0 2.4 %collective-permute-done.8 = f32[8,3072]{1,0:T(8,128)S(1)} collective-permute-done((f32[8,3072]{1,0:T(8,128)S(1)}, f32[8,3072]{1,0:T(8,128)S(1)}, u32[]{:S(2)}, u32[]{:S(2)}) %collective-permute-start.8) | collective-permute-done | bytes 98336 | tf_op jit(solution)/shard_map/ppermute | solution.py:113
  126.4 1.0 copy.37
  (16 shorter events, 0.2 us)
Async XLA Ops:
  6.5 37.8 %copy-start = (f32[128,512]{1,0:T(8,128)S(1)}, f32[128,512]{1,0:T(8,128)}, u32[]{:S(2)}) copy-start(f32[128,512]{1,0:T(8,128)} %param.16) | copy-start | bytes 786436
  6.5 16.5 %copy-start.1 = (f32[8,64,384]{2,1,0:T(8,128)S(1)}, f32[8,64,384]{2,1,0:T(8,128)}, u32[]{:S(2)}) copy-start(f32[8,64,384]{2,1,0:T(8,128)} %param.9) | copy-start | bytes 2359300
  7.6 11.5 %collective-permute-start = (f32[9,2,384]{2,1,0:T(2,128)S(1)}, f32[9,2,384]{2,1,0:T(2,128)S(1)}, u32[]{:S(2)}, u32[]{:S(2)}) collective-permute-start(f32[9,2,384]{2,1,0:T(2,128)S(1)} %get-tuple-element.10), channel_id=1, source_target_pairs={{1,0},{2,1},{3,2},{5,4},{6,5},{7,6},{9,8},{10,9},{11,10},{13,12},{... | collective-permute-start | bytes 82952 | tf_op jit(solution)/shard_map/ppermute | solution.py:15
  8.9 11.1 %collective-permute-start.1 = (f32[9,2,384]{2,1,0:T(2,128)S(1)}, f32[9,2,384]{2,1,0:T(2,128)S(1)}, u32[]{:S(2)}, u32[]{:S(2)}) collective-permute-start(f32[9,2,384]{2,1,0:T(2,128)S(1)} %get-tuple-element.9), channel_id=1, source_target_pairs={{0,1},{1,2},{2,3},{4,5},{5,6},{6,7},{8,9},{9,10},{10,11},{12,13},{... | collective-permute-start | bytes 82952 | tf_op jit(solution)/shard_map/ppermute | solution.py:12
  21.7 9.9 %copy-start.2 = (s32[128,4]{0,1:T(4,128)S(1)}, s32[128,4]{0,1:T(4,128)}, u32[]{:S(2)}) copy-start(s32[128,4]{0,1:T(4,128)} %param.13) | copy-start | bytes 6148
  24.8 64.1 %all-to-all-start = ((f32[8,8,3072]{2,0,1:T(8,128)}), f32[8,8,3072]{2,0,1:T(8,128)S(1)}, u32[]{:S(2)}, u32[]{:S(2)}) async-start(f32[8,8,3072]{2,0,1:T(8,128)} %copy.30), calls=%async_computation | async-start | bytes 1572864 | tf_op jit(solution)/shard_map/all_to_all | solution.py:80
  30.9 37.6 %reduce-scatter.2.cloned.1.call-start = ((), (), s32[]{:S(2)}) async-start(), calls=%async_computation.2 | async-start | bytes 20480 | tf_op jit(solution)/shard_map/reduce_scatter | solution.py:74
  31.8 12.5 %copy-start.3 = (f32[8,128]{1,0:T(8,128)S(1)}, f32[8,128]{1,0:T(8,128)}, u32[]{:S(2)}) copy-start(f32[8,128]{1,0:T(8,128)} %param.15) | copy-start | bytes 12292
  31.8 12.5 %copy-start.4 = (f32[128]{0:T(128)S(1)}, f32[128]{0:T(128)}, u32[]{:S(2)}) copy-start(f32[128]{0:T(128)} %param.14) | copy-start | bytes 1540
  100.4 8.2 %collective-permute-start.2 = (f32[8,3072]{1,0:T(8,128)S(1)}, f32[8,3072]{1,0:T(8,128)S(1)}, u32[]{:S(2)}, u32[]{:S(2)}) collective-permute-start(f32[8,3072]{1,0:T(8,128)S(1)} %get-tuple-element.17), channel_id=1, source_target_pairs={{0,4},{4,0},{8,12},{12,8},{16,20},{20,16},{24,28},{28,24},{1,5},{5... | collective-permute-start | bytes 294920 | tf_op jit(solution)/shard_map/ppermute | solution.py:113
  102.7 6.5 %collective-permute-start.3 = (f32[8,3072]{1,0:T(8,128)S(1)}, f32[8,3072]{1,0:T(8,128)S(1)}, u32[]{:S(2)}, u32[]{:S(2)}) collective-permute-start(f32[8,3072]{1,0:T(8,128)S(1)} %get-tuple-element.16), channel_id=1, source_target_pairs={{0,8},{4,12},{8,0},{12,4},{16,24},{20,28},{24,16},{28,20},{1,9},{5... | collective-permute-start | bytes 294920 | tf_op jit(solution)/shard_map/ppermute | solution.py:113
  105.6 5.5 %collective-permute-start.4 = (f32[8,3072]{1,0:T(8,128)S(1)}, f32[8,3072]{1,0:T(8,128)S(1)}, u32[]{:S(2)}, u32[]{:S(2)}) collective-permute-start(f32[8,3072]{1,0:T(8,128)S(1)} %get-tuple-element.15), channel_id=1, source_target_pairs={{0,12},{4,8},{8,4},{12,0},{16,28},{20,24},{24,20},{28,16},{1,13},{... | collective-permute-start | bytes 294920 | tf_op jit(solution)/shard_map/ppermute | solution.py:113
  105.7 7.2 %collective-permute-start.5 = (f32[8,3072]{1,0:T(8,128)S(1)}, f32[8,3072]{1,0:T(8,128)S(1)}, u32[]{:S(2)}, u32[]{:S(2)}) collective-permute-start(f32[8,3072]{1,0:T(8,128)S(1)} %get-tuple-element.14), channel_id=1, source_target_pairs={{0,16},{4,20},{8,24},{12,28},{16,0},{20,4},{24,8},{28,12},{1,17},{... | collective-permute-start | bytes 294920 | tf_op jit(solution)/shard_map/ppermute | solution.py:113
  106.5 13.1 %collective-permute-start.6 = (f32[8,3072]{1,0:T(8,128)S(1)}, f32[8,3072]{1,0:T(8,128)S(1)}, u32[]{:S(2)}, u32[]{:S(2)}) collective-permute-start(f32[8,3072]{1,0:T(8,128)S(1)} %get-tuple-element.13), channel_id=1, source_target_pairs={{0,20},{4,16},{8,28},{12,24},{16,4},{20,0},{24,12},{28,8},{1,21},{... | collective-permute-start | bytes 294920 | tf_op jit(solution)/shard_map/ppermute | solution.py:113
  108.6 15.4 %collective-permute-start.7 = (f32[8,3072]{1,0:T(8,128)S(1)}, f32[8,3072]{1,0:T(8,128)S(1)}, u32[]{:S(2)}, u32[]{:S(2)}) collective-permute-start(f32[8,3072]{1,0:T(8,128)S(1)} %get-tuple-element.12), channel_id=1, source_target_pairs={{0,24},{4,28},{8,16},{12,20},{16,8},{20,12},{24,0},{28,4},{1,25},{... | collective-permute-start | bytes 294920 | tf_op jit(solution)/shard_map/ppermute | solution.py:113
  109.2 17.2 %collective-permute-start.8 = (f32[8,3072]{1,0:T(8,128)S(1)}, f32[8,3072]{1,0:T(8,128)S(1)}, u32[]{:S(2)}, u32[]{:S(2)}) collective-permute-start(f32[8,3072]{1,0:T(8,128)S(1)} %get-tuple-element.11), channel_id=1, source_target_pairs={{0,28},{4,24},{8,20},{12,16},{16,12},{20,8},{24,4},{28,0},{1,29},{... | collective-permute-start | bytes 294920 | tf_op jit(solution)/shard_map/ppermute | solution.py:113
Sparse Core Ops, SparseCore 0:
  45.4 23.1 reduce-scatter.1
